TPU v7x, 32 devices: a whole 2x2x4 slice. The times are simulated.
32 devices in a mesh: grp: 2 (over x), yz: 8 (over z, y), gx: 2 (over core).
Axes of the slice: x: 2, y: 2, z: 4, core: 2. Of those that a mesh axis runs over, the one named last changes fastest.
Arguments:
- field: bfloat16 [4096, 256, 128], P(('grp', 'gx'), 'yz'), parts along dimension 0, may hold values from -6 to 6
- sketch_seeds: int32 [12], P('grp'), parts along dimension 0, may hold values from 1 to 32748
Outputs:
- basis: float32 [4096, 256], P(('grp', 'gx')), parts along dimension 0
- core: bfloat16 [512, 256, 128], P(('grp', 'gx'), 'yz'), parts along dimension 0
There are 2 independent parts, one for each index of `grp`. A program takes and returns all parts, laid end to end along the dimension named above; each array names one. Nothing has to cross between parts.
All inputs are finite; a program needn't handle non-finite values.
Results may differ from a plain program's by a relative error of at most 0.0057.
Values sent between devices are 32-bit elements; how exact they have to be, the bound alone decides.
No kernel may reach another device: no remote copies, remote signals or barrier semaphores. Data moves between devices by JAX's collectives and lax.ppermute only.
A program may use at most 64 MiB of HBM per device.

v0:
```python
import math
import jax
import jax.numpy as jnp
from jax import lax
from jax.sharding import PartitionSpec as P

RANK = 256
prime = 32749


def omega_table(seeds, start, count):
    place = (start + jnp.arange(count, dtype=jnp.int32) + 1)[:, None]
    column = (jnp.arange(RANK, dtype=jnp.int32) + 1)[None, :]
    first = seeds[0] * place % prime
    second = (seeds[1] * column + seeds[2]) % prime
    square = place * place % prime
    third = seeds[2] * column % prime
    mixed = (first * second % prime + square * third % prime) % prime
    return mixed.astype(jnp.float32) * (2.0 / prime) - 1.0


def local(field, sketch_seeds):
    x_local, y_local, z_local = field.shape
    y_start = lax.axis_index("yz") * y_local
    omega_z = omega_table(sketch_seeds[3:6], 0, z_local).astype(jnp.bfloat16)
    omega_y = omega_table(sketch_seeds[0:3], y_start, y_local)
    block = math.gcd(y_local, 8)

    def add_block(total, index):
        rows = lax.dynamic_slice_in_dim(field, index * block, block, 1)
        proj = jnp.dot(
            rows.reshape(x_local * block, z_local), omega_z, preferred_element_type=jnp.float32
        ).reshape(x_local, block, RANK)
        weight_y = lax.dynamic_slice_in_dim(omega_y, index * block, block, 0)
        return (total + jnp.sum(proj * weight_y[None], axis=1), None)

    partial_value, unused = lax.scan(
        add_block,
        jnp.zeros((x_local, RANK), jnp.float32),
        jnp.arange(y_local // block, dtype=jnp.int32),
    )
    sketch = lax.psum(partial_value, "yz")
    gram = lax.psum(
        jnp.dot(
            sketch.T, sketch, precision=lax.Precision.HIGHEST, preferred_element_type=jnp.float32
        ),
        "gx",
    )
    lower = jnp.linalg.cholesky(gram)
    basis = lax.linalg.triangular_solve(
        lower, sketch, left_side=False, lower=True, transpose_a=True
    )
    basis_half = basis.astype(jnp.bfloat16)
    flat = field.reshape(x_local, y_local * z_local)
    owned_rank = RANK // lax.axis_size("gx")
    core = lax.psum_scatter(
        lax.dot_general(
            basis_half, flat, (((0,), (0,)), ((), ())), preferred_element_type=jnp.float32
        ),
        "gx",
        scatter_dimension=0,
        tiled=True,
    )
    return (basis, core.reshape(owned_rank, y_local, z_local).astype(jnp.bfloat16))


def solution(mesh):
    in_specs = (P(("grp", "gx"), "yz", None), P("grp"))
    out_specs = (P(("grp", "gx"), None), P(("grp", "gx"), "yz", None))
    return jax.shard_map(local, mesh=mesh, in_specs=in_specs, out_specs=out_specs, check_vma=False)
```

profile of v0, /device:TPU:0, one launch (start us, length us, event | category | flops | bytes accessed | tf_op | source)
XLA Modules:
  0.0 233.7 jit_solution(5224184737601147460)
XLA Ops:
  7.2 0.0 all-reduce.4.cloned.1.call-start
  7.2 1.6 fusion.53
  8.8 0.7 and_select_fusion.5
  9.5 0.6 and_select_fusion.1
  10.1 1.3 and_select_fusion.4
  11.4 1.2 and_select_fusion
  12.6 0.1 fusion.45
  12.8 20.5 %while.13 = (s32[]{:T(128)}, f32[1024,256]{1,0:T(8,128)S(1)}, s32[4]{0:T(128)S(1)}, bf16[1024,32,128]{2,1,0:T(8,128)(2,1)}, f32[32,256]{1,0:T(8,128)S(1)}, /*ind...) while((s32[]{:T(128)}, f32[1024,256]{1,0:T(8,128)S(1)}, ...), condition=%wide.region_2.3_spmd.clone, body=%wide.region_0.2_spmd.clone.sunk | while | flops 542146560 | bytes 10513617 | solution.py:37
  12.8 0.7 dynamic_slice.20
  14.1 1.7 constant_dynamic-slice_fusion.8
  15.9 1.7 multiply_reduce_fusion.2
  17.6 0.3 select_add_fusion.2
  17.9 0.7 dynamic_slice.20
  19.3 1.7 constant_dynamic-slice_fusion.8
  21.0 1.7 multiply_reduce_fusion.2
  22.7 0.3 select_add_fusion.2
  23.0 0.7 dynamic_slice.20
  24.4 1.7 constant_dynamic-slice_fusion.8
  26.1 1.7 multiply_reduce_fusion.2
  27.9 0.3 select_add_fusion.2
  28.2 0.7 dynamic_slice.20
  29.5 1.7 constant_dynamic-slice_fusion.8
  31.3 1.7 multiply_reduce_fusion.2
  33.0 0.3 select_add_fusion.2
  33.3 0.0 copy-start
  33.3 1.0 copy-done
  34.2 0.0 all-reduce.4.cloned.1.call-update
  34.3 0.0 all-reduce.6.cloned.1.call-start
  34.3 81.1 %all-reduce.4.cloned.1.call-done = f32[1024,256]{1,0:T(8,128)} async-done(((f32[1024,256]{1,0:T(8,128)}), f32[1024,256]{1,0:T(8,128)}) %all-reduce.4.cloned.1.call-update) | async-done | bytes 1048592 | tf_op jit(solution)/shard_map/psum | solution.py:42
  115.4 0.0 copy-start.1
  115.4 4.1 %fusion.54 = f32[256,256]{0,1:T(8,128)} fusion(f32[1024,256]{1,0:T(8,128)} %all-reduce.4.cloned.1.call-done), kind=kOutput, calls=%fused_computation.98 | convolution fusion | flops 805306368 | bytes 1310720 | tf_op jit(solution)/shard_map/dot_general | solution.py:44
  119.6 0.0 all-reduce.6.cloned.1.call-update
  119.6 0.2 reduce-scatter.2.cloned.1.call-start
  119.8 17.7 %all-reduce.6.cloned.1.call-done = f32[256,256]{0,1:T(8,128)} async-done(((f32[256,256]{0,1:T(8,128)}), f32[256,256]{0,1:T(8,128)}) %all-reduce.6.cloned.1.call-update) | async-done | bytes 262160 | tf_op jit(solution)/shard_map/psum | solution.py:43
  137.6 1.1 copy.6
  138.6 1.0 fusion.35
  139.6 11.7 %cholesky.50 = f32[128,128]{1,0:T(8,128)S(1)} custom-call(f32[128,128]{1,0:T(8,128)S(1)} %cholesky.118), custom_call_target="Cholesky" | custom-call | tf_op jit(solution)/shard_map/jit(cholesky)/cholesky | solution.py:49
  151.4 0.6 compare_reduce_fusion.1
  152.0 9.8 %custom-call.14 = f32[1,128,128]{1,2,0:T(8,128)S(1)} custom-call(f32[1,128,128]{2,1,0:T(8,128)S(1)} %get-tuple-element.121), custom_call_target="InvertDiagBlocksLowerTriangular" | custom-call | tf_op jit(solution)/shard_map/jit(cholesky)/cholesky | solution.py:49
  161.9 0.2 constant_dynamic-update-slice_fusion.1
  162.1 0.3 convolution_subtract_fusion.1
  162.4 11.7 %cholesky.105 = f32[128,128]{1,0:T(8,128)S(1)} custom-call(f32[128,128]{1,0:T(8,128)S(1)} %convolution_subtract_fusion.1), custom_call_target="Cholesky" | custom-call | tf_op jit(solution)/shard_map/jit(cholesky)/cholesky | solution.py:49
  174.1 0.7 compare_reduce_fusion
  176.2 0.1 triangular_solve.58
  176.3 4.3 %while.12 = (s32[]{:T(128)}, f32[256,256]{1,0:T(8,128)S(1)}, s32[2,2]{1,0:T(2,128)S(1)}, f32[2,128,128]{2,1,0:T(8,128)S(1)}, s32[]{:T(128)}) while((s32[]{:T(128)}, f32[256,256]{1,0:T(8,128)S(1)}, s32[2,2]{1,0:T(2,128)S(1)}, f32[2,128,128]{2,1,0:T(8,128)S(1)}, s32[]{:T(128)}) %tuple.57), condition=%wide.while_cond, body=%wide.while_body.sunk | while | flops 2 | bytes 131189 | solution.py:50
  176.5 0.6 fusion.64
  177.1 1.4 bitcast_dynamic-update-slice_fusion.2
  178.5 0.6 fusion.64
  179.1 1.4 bitcast_dynamic-update-slice_fusion.2
  180.5 19.7 %custom-call.15 = f32[2,128,128]{1,2,0:T(8,128)S(1)} custom-call(f32[2,128,128]{2,1,0:T(8,128)S(1)} %get-tuple-element.42), custom_call_target="InvertDiagBlocksLowerTriangular" | custom-call | tf_op jit(solution)/shard_map/triangular_solve | solution.py:50
  200.2 0.0 copy-done.1
  200.2 0.6 fusion.32
  200.9 1.0 convolution_subtract_fusion
  201.9 0.6 fusion.36
  202.5 8.3 %fusion.29 = f32[256,4096]{1,0:T(8,128)} fusion(bf16[128,8,32,128]{3,2,1,0:T(8,128)(2,1)} %bitcast.54, f32[1024,128]{0,1:T(8,128)S(1)} %fusion.36, f32[1024,128]{0,1:T(8,128)S(1)} %fusion.32), kind=kOutput, calls=%fused_computation.38 | convolution fusion | flops 2148532224 | bytes 13631488 | tf_op jit(solution)/shard_map/dot_general | solution.py:57
  210.8 0.0 reduce-scatter.2.cloned.1.call-update
  210.8 0.1 pad_maximum_fusion
  210.9 1.3 copy.7
  212.2 12.0 %reduce-scatter.2.cloned.1.call-done = f32[128,4096]{1,0:T(8,128)} async-done(((f32[256,4096]{1,0:T(8,128)}), f32[128,4096]{1,0:T(8,128)}) %reduce-scatter.2.cloned.1.call-update) | async-done | bytes 2097168 | tf_op jit(solution)/shard_map/reduce_scatter | solution.py:56
  224.2 1.8 convert_bitcast_fusion
  226.0 1.2 copy.11
  (15 shorter events, 0.2 us)
Async XLA Ops:
  7.2 108.2 %all-reduce.4.cloned.1.call-start = ((), (), s32[]{:S(2)}) async-start(), calls=%async_computation.1 | async-start | bytes 2097152 | tf_op jit(solution)/shard_map/psum | solution.py:42
  33.3 1.0 copy-start
  34.3 103.3 %all-reduce.6.cloned.1.call-start = ((), (), s32[]{:S(2)}) async-start(), calls=%async_computation.2 | async-start | bytes 524288 | tf_op jit(solution)/shard_map/psum | solution.py:43
  115.4 84.8 %copy-start.1 = (f32[1024,256]{1,0:T(8,128)S(1)}, f32[1024,256]{1,0:T(8,128)}, u32[]{:S(2)}) copy-start(f32[1024,256]{1,0:T(8,128)} %all-reduce.4.cloned.1.call-done) | copy-start | bytes 3145732
  119.6 104.6 %reduce-scatter.2.cloned.1.call-start = ((), (), s32[]{:S(2)}) async-start(), calls=%async_computation.3 | async-start | bytes 6291456 | tf_op jit(solution)/shard_map/reduce_scatter | solution.py:56
Sparse Core Ops, SparseCore 0:
  34.4 80.9 all-reduce.3
  119.7 17.8 all-reduce.5
  210.9 13.2 reduce-scatter.1
where the time goes:
time: 234 us
  waiting for transfers between devices  111 us (47%)
  other arithmetic  62.3 us (27%)
  matrix products  21.9 us (9%)
  local copies, waits for them, and re-layouts  19.9 us (9%)
  between operations  15.3 us (7%)
  loops' own time  3.19 us (1%)
    psum x1, waiting for transfers between devices, local(): sketch = lax.psum(partial_value, 'yz')  81.1 us
    another operation x7, other arithmetic, local(): lower = jnp.linalg.cholesky(gram)  34.7 us
    another operation x4, other arithmetic, local(): lax.linalg.triangular_solve(lower, sketch, left_side=False, lower=True, t...  19.8 us
    psum x1, waiting for transfers between devices, local(): lax.psum(jnp.dot(sketch.T, sketch, precision=lax.Precision.HIGHEST, prefe...  17.7 us
    reduce_scatter x1, waiting for transfers between devices, local(): lax.psum_scatter(lax.dot_general(basis_half, flat, (((0,), (0,)), ((), ()...  12 us
    dot_general x1, matrix products, local(): lax.dot_general(basis_half, flat, (((0,), (0,)), ((), ())), preferred_ele...  8.29 us
    dynamic_slice x4, local copies, waits for them, and re-layouts, add_block(): rows = lax.dynamic_slice_in_dim(field, index * block, block, 1)  6.93 us
    dot_general x4, matrix products, add_block(): jnp.dot(rows.reshape(x_local * block, z_local), omega_z, preferred_elemen...  6.81 us
  transfers between devices with their start and end apart: 3, of which 3 were waited for; matrix products, arithmetic and copies ran while one was open for 1% of the time, Pallas kernels for 0%

commit v1 on v0

--- a/solution.py
+++ b/solution.py
@@ -39,7 +39,9 @@
         jnp.zeros((x_local, RANK), jnp.float32),
         jnp.arange(y_local // block, dtype=jnp.int32),
     )
-    sketch = lax.psum(partial_value, "yz")
+    sketch = partial_value
+    for hop in (1, 2, 4):
+        sketch = sketch + lax.ppermute(sketch, "yz", [(dev, dev ^ hop) for dev in range(8)])
     gram = lax.psum(
         jnp.dot(
             sketch.T, sketch, precision=lax.Precision.HIGHEST, preferred_element_type=jnp.float32

time: 234 us -> 250 us (1.068)
  waiting for transfers between devices: 111 us -> 121 us
  starting transfers between devices: 0.3 us -> 7.62 us
    ppermute x0 -> x3, waiting for transfers between devices: none -> 90.2 us  [local(): lax.ppermute(sketch, 'yz', [(dev, dev ^ hop) for dev in range(8)])]
    psum x1 -> x0, waiting for transfers between devices: 81.1 us -> none  [local(): sketch = lax.psum(partial_value, 'yz')]
    ppermute x0 -> x3, starting transfers between devices: none -> 7.36 us  [local(): lax.ppermute(sketch, 'yz', [(dev, dev ^ hop) for dev in range(8)])]
  transfers between devices with their start and end apart: 3 -> 5, of which waited for: 3 -> 5; matrix products, arithmetic and copies ran while one was open for 1% -> 1% of each run, Pallas kernels for 0% -> 0%
where the time goes in v1:
time: 250 us; the launch traced here: 249 us
  waiting for transfers between devices  121 us (48%)
  other arithmetic  62.7 us (25%)
  matrix products  20.4 us (8%)
  local copies, waits for them, and re-layouts  18.9 us (8%)
  between operations  15.6 us (6%)
  starting transfers between devices  7.62 us (3%)
  loops' own time  3.19 us (1%)
    ppermute x3, waiting for transfers between devices, local(): lax.ppermute(sketch, 'yz', [(dev, dev ^ hop) for dev in range(8)])  90.2 us
    another operation x7, other arithmetic, local(): lower = jnp.linalg.cholesky(gram)  34.7 us
    another operation x4, other arithmetic, local(): lax.linalg.triangular_solve(lower, sketch, left_side=False, lower=True, t...  19.8 us
    psum x1, waiting for transfers between devices, local(): lax.psum(jnp.dot(sketch.T, sketch, precision=lax.Precision.HIGHEST, prefe...  18.9 us
    reduce_scatter x1, waiting for transfers between devices, local(): lax.psum_scatter(lax.dot_general(basis_half, flat, (((0,), (0,)), ((), ()...  12 us
    dot_general x1, matrix products, local(): lax.dot_general(basis_half, flat, (((0,), (0,)), ((), ())), preferred_ele...  8.3 us
    ppermute x3, starting transfers between devices, local(): lax.ppermute(sketch, 'yz', [(dev, dev ^ hop) for dev in range(8)])  7.36 us
    dynamic_slice x4, local copies, waits for them, and re-layouts, add_block(): rows = lax.dynamic_slice_in_dim(field, index * block, block, 1)  6.93 us
  transfers between devices with their start and end apart: 5, of which 5 were waited for; matrix products, arithmetic and copies ran while one was open for 1% of the time, Pallas kernels for 0%

profile of v1, /device:TPU:0, one launch (start us, length us, event | category | flops | bytes accessed | tf_op | source)
XLA Modules:
  0.0 249.4 jit_solution(11131254630655246790)
XLA Ops:
  7.2 0.0 all-reduce.3.cloned.1.call-start
  7.2 1.6 fusion.54
  8.8 0.7 and_select_fusion.5
  9.5 0.6 and_select_fusion.1
  10.1 1.3 and_select_fusion.4
  11.4 1.2 and_select_fusion
  12.6 0.1 fusion.46
  12.8 20.5 %while.13 = (s32[]{:T(128)}, f32[1024,256]{1,0:T(8,128)S(1)}, s32[4]{0:T(128)S(1)}, bf16[1024,32,128]{2,1,0:T(8,128)(2,1)}, f32[32,256]{1,0:T(8,128)S(1)}, /*ind...) while((s32[]{:T(128)}, f32[1024,256]{1,0:T(8,128)S(1)}, ...), condition=%wide.region_2.3_spmd.clone, body=%wide.region_0.2_spmd.clone.sunk | while | flops 542146560 | bytes 10513617 | solution.py:37
  12.8 0.7 dynamic_slice.20
  14.1 1.7 constant_dynamic-slice_fusion.8
  15.9 1.7 multiply_reduce_fusion.2
  17.6 0.3 select_add_fusion.2
  17.9 0.7 dynamic_slice.20
  19.3 1.7 constant_dynamic-slice_fusion.8
  21.0 1.7 multiply_reduce_fusion.2
  22.7 0.3 select_add_fusion.2
  23.0 0.7 dynamic_slice.20
  24.4 1.7 constant_dynamic-slice_fusion.8
  26.1 1.7 multiply_reduce_fusion.2
  27.9 0.3 select_add_fusion.2
  28.2 0.7 dynamic_slice.20
  29.5 1.7 constant_dynamic-slice_fusion.8
  31.3 1.7 multiply_reduce_fusion.2
  33.0 0.3 select_add_fusion.2
  33.3 3.0 %collective-permute-start = (f32[1024,256]{1,0:T(8,128)S(1)}, f32[1024,256]{1,0:T(8,128)S(1)}, u32[]{:S(2)}, u32[]{:S(2)}) collective-permute-start(f32[1024,256]{1,0:T(8,128)S(1)} %get-tuple-element.34), channel_id=1, source_target_pairs={{0,2},{2,0},{4,6},{6,4},{8,10},{10,8},{12,14},{14,12},{1,3},{3,1},... | collective-permute-start | bytes 3145736 | tf_op jit(solution)/shard_map/ppermute | solution.py:44
  36.3 23.2 %collective-permute-done = f32[1024,256]{1,0:T(8,128)S(1)} collective-permute-done((f32[1024,256]{1,0:T(8,128)S(1)}, f32[1024,256]{1,0:T(8,128)S(1)}, u32[]{:S(2)}, u32[]{:S(2)}) %collective-permute-start) | collective-permute-done | bytes 1048608 | tf_op jit(solution)/shard_map/ppermute | solution.py:44
  59.5 0.1 add.272
  59.6 1.8 collective-permute-start.1
  61.5 22.6 %collective-permute-done.1 = f32[1024,256]{1,0:T(8,128)S(1)} collective-permute-done((f32[1024,256]{1,0:T(8,128)S(1)}, f32[1024,256]{1,0:T(8,128)S(1)}, u32[]{:S(2)}, u32[]{:S(2)}) %collective-permute-start.1) | collective-permute-done | bytes 1048608 | tf_op jit(solution)/shard_map/ppermute | solution.py:44
  84.0 0.1 add.273
  84.2 2.5 %collective-permute-start.2 = (f32[1024,256]{1,0:T(8,128)S(1)}, f32[1024,256]{1,0:T(8,128)S(1)}, u32[]{:S(2)}, u32[]{:S(2)}) collective-permute-start(f32[1024,256]{1,0:T(8,128)S(1)} %add.273), channel_id=1, source_target_pairs={{0,8},{2,10},{4,12},{6,14},{8,0},{10,2},{12,4},{14,6},{1,9},{3,11}... | collective-permute-start | bytes 3145736 | tf_op jit(solution)/shard_map/ppermute | solution.py:44
  86.7 44.4 %collective-permute-done.2 = f32[1024,256]{1,0:T(8,128)S(1)} collective-permute-done((f32[1024,256]{1,0:T(8,128)S(1)}, f32[1024,256]{1,0:T(8,128)S(1)}, u32[]{:S(2)}, u32[]{:S(2)}) %collective-permute-start.2) | collective-permute-done | bytes 1048608 | tf_op jit(solution)/shard_map/ppermute | solution.py:44
  131.1 0.1 add.274
  131.3 2.5 %fusion.55 = f32[256,256]{0,1:T(8,128)} fusion(f32[1024,256]{1,0:T(8,128)S(1)} %add.274), kind=kOutput, calls=%fused_computation.99 | convolution fusion | flops 805306368 | bytes 1310720 | tf_op jit(solution)/shard_map/dot_general | solution.py:46
  133.8 0.0 all-reduce.3.cloned.1.call-update
  133.8 0.2 reduce-scatter.2.cloned.1.call-start
  134.0 18.9 %all-reduce.3.cloned.1.call-done = f32[256,256]{0,1:T(8,128)} async-done(((f32[256,256]{0,1:T(8,128)}), f32[256,256]{0,1:T(8,128)}) %all-reduce.3.cloned.1.call-update) | async-done | bytes 262160 | tf_op jit(solution)/shard_map/psum | solution.py:45
  153.0 1.1 copy.6
  154.0 1.0 fusion.36
  155.0 11.7 %cholesky.50 = f32[128,128]{1,0:T(8,128)S(1)} custom-call(f32[128,128]{1,0:T(8,128)S(1)} %cholesky.118), custom_call_target="Cholesky" | custom-call | tf_op jit(solution)/shard_map/jit(cholesky)/cholesky | solution.py:51
  166.8 0.6 compare_reduce_fusion.1
  167.4 9.8 %custom-call.14 = f32[1,128,128]{1,2,0:T(8,128)S(1)} custom-call(f32[1,128,128]{2,1,0:T(8,128)S(1)} %get-tuple-element.121), custom_call_target="InvertDiagBlocksLowerTriangular" | custom-call | tf_op jit(solution)/shard_map/jit(cholesky)/cholesky | solution.py:51
  177.3 0.2 constant_dynamic-update-slice_fusion.1
  177.5 0.3 convolution_subtract_fusion
  177.7 11.7 %cholesky.105 = f32[128,128]{1,0:T(8,128)S(1)} custom-call(f32[128,128]{1,0:T(8,128)S(1)} %convolution_subtract_fusion), custom_call_target="Cholesky" | custom-call | tf_op jit(solution)/shard_map/jit(cholesky)/cholesky | solution.py:51
  189.5 0.7 compare_reduce_fusion
  191.6 0.1 triangular_solve.58
  191.7 4.3 %while.12 = (s32[]{:T(128)}, f32[256,256]{1,0:T(8,128)S(1)}, s32[2,2]{1,0:T(2,128)S(1)}, f32[2,128,128]{2,1,0:T(8,128)S(1)}, s32[]{:T(128)}) while((s32[]{:T(128)}, f32[256,256]{1,0:T(8,128)S(1)}, s32[2,2]{1,0:T(2,128)S(1)}, f32[2,128,128]{2,1,0:T(8,128)S(1)}, s32[]{:T(128)}) %tuple.57), condition=%wide.while_cond, body=%wide.while_body.sunk | while | flops 2 | bytes 131189 | solution.py:52
  191.9 0.6 fusion.64
  192.5 1.4 bitcast_dynamic-update-slice_fusion.2
  193.9 0.6 fusion.64
  194.5 1.4 bitcast_dynamic-update-slice_fusion.2
  195.9 19.7 %custom-call.15 = f32[2,128,128]{1,2,0:T(8,128)S(1)} custom-call(f32[2,128,128]{2,1,0:T(8,128)S(1)} %get-tuple-element.42), custom_call_target="InvertDiagBlocksLowerTriangular" | custom-call | tf_op jit(solution)/shard_map/triangular_solve | solution.py:52
  215.6 0.6 fusion.33
  216.2 1.0 fusion.37
  217.2 0.6 fusion.32
  217.9 8.3 %fusion.29 = f32[256,4096]{1,0:T(8,128)} fusion(bf16[128,8,32,128]{3,2,1,0:T(8,128)(2,1)} %bitcast.53, f32[1024,128]{0,1:T(8,128)S(1)} %fusion.32, f32[1024,128]{0,1:T(8,128)S(1)} %fusion.33), kind=kOutput, calls=%fused_computation.38 | convolution fusion | flops 2148532224 | bytes 13631488 | tf_op jit(solution)/shard_map/dot_general | solution.py:59
  226.2 0.0 reduce-scatter.2.cloned.1.call-update
  226.2 0.1 pad_maximum_fusion
  226.3 1.3 copy.7
  227.6 12.0 %reduce-scatter.2.cloned.1.call-done = f32[128,4096]{1,0:T(8,128)} async-done(((f32[256,4096]{1,0:T(8,128)}), f32[128,4096]{1,0:T(8,128)}) %reduce-scatter.2.cloned.1.call-update) | async-done | bytes 2097168 | tf_op jit(solution)/shard_map/reduce_scatter | solution.py:58
  239.6 1.8 convert_bitcast_fusion
  241.4 1.2 copy.11
  (15 shorter events, 0.2 us)
Async XLA Ops:
  7.2 145.8 %all-reduce.3.cloned.1.call-start = ((), (), s32[]{:S(2)}) async-start(), calls=%async_computation.1 | async-start | bytes 524288 | tf_op jit(solution)/shard_map/psum | solution.py:45
  33.3 26.2 %collective-permute-start = (f32[1024,256]{1,0:T(8,128)S(1)}, f32[1024,256]{1,0:T(8,128)S(1)}, u32[]{:S(2)}, u32[]{:S(2)}) collective-permute-start(f32[1024,256]{1,0:T(8,128)S(1)} %get-tuple-element.34), channel_id=1, source_target_pairs={{0,2},{2,0},{4,6},{6,4},{8,10},{10,8},{12,14},{14,12},{1,3},{3,1},... | collective-permute-start | bytes 3145736 | tf_op jit(solution)/shard_map/ppermute | solution.py:44
  59.6 24.4 %collective-permute-start.1 = (f32[1024,256]{1,0:T(8,128)S(1)}, f32[1024,256]{1,0:T(8,128)S(1)}, u32[]{:S(2)}, u32[]{:S(2)}) collective-permute-start(f32[1024,256]{1,0:T(8,128)S(1)} %add.272), channel_id=1, source_target_pairs={{0,4},{2,6},{4,0},{6,2},{8,12},{10,14},{12,8},{14,10},{1,5},{3,7},... | collective-permute-start | bytes 3145736 | tf_op jit(solution)/shard_map/ppermute | solution.py:44
  84.2 46.9 %collective-permute-start.2 = (f32[1024,256]{1,0:T(8,128)S(1)}, f32[1024,256]{1,0:T(8,128)S(1)}, u32[]{:S(2)}, u32[]{:S(2)}) collective-permute-start(f32[1024,256]{1,0:T(8,128)S(1)} %add.273), channel_id=1, source_target_pairs={{0,8},{2,10},{4,12},{6,14},{8,0},{10,2},{12,4},{14,6},{1,9},{3,11}... | collective-permute-start | bytes 3145736 | tf_op jit(solution)/shard_map/ppermute | solution.py:44
  133.8 105.8 %reduce-scatter.2.cloned.1.call-start = ((), (), s32[]{:S(2)}) async-start(), calls=%async_computation.2 | async-start | bytes 6291456 | tf_op jit(solution)/shard_map/reduce_scatter | solution.py:58
Sparse Core Ops, SparseCore 0:
  133.9 18.9 all-reduce.2
  226.3 13.2 reduce-scatter.1
